TPU v7x, 512 devices: a whole 4x4x16 slice. The times are simulated.
512 devices in a mesh: mode: 64 (over y, z), rank: 8 (over x, core).
Axes of the slice: x: 4, y: 4, z: 16, core: 2. Of those that a mesh axis runs over, the one named last changes fastest.
Arguments:
- operator_cores: bfloat16 [2, 4, 4, 2048, 2048], P(None, None, None, 'mode'), may hold values from -0.26516504 to 0.26516504
- vector_cores: bfloat16 [2, 64, 64, 2048], P(None, 'rank', None, 'mode'), may hold values from -17 to 17
- left_gram: float32 [256, 256], replicated, may hold values from -330 to 330, as said below
- bases: float32 [3, 256, 64], replicated, may hold values from -0.375 to 0.375
Outputs:
- rounded_cores: float32 [2, 64, 2048, 64], P(None, None, ('mode', 'rank'))
- final_gram: float32 [256, 256], replicated
Inputs may be any that keep to these rules, and one draw needn't show every extreme that they name: left_gram is symmetric positive definite.
All inputs are finite; a program needn't handle non-finite values.
Results may differ from a plain program's by a relative error of at most 0.0028.
Values may be sent and summed in bfloat16 or wider, within the bound.
A program may use at most 64 MiB of HBM per device.

v0:
```python
import jax
import jax.numpy as jnp
from jax import lax
from jax.sharding import PartitionSpec as P

MODES = 2048
RANK = 256
HIGHEST_PRECISION = lax.Precision.HIGHEST


def solve_mixing(gram_now, basis):
    projected = jnp.dot(
        basis.T, gram_now, precision=HIGHEST_PRECISION, preferred_element_type=jnp.float32
    )
    reduced = jnp.dot(
        projected, basis, precision=HIGHEST_PRECISION, preferred_element_type=jnp.float32
    )
    reduced = 0.5 * (reduced + reduced.T)
    lower_factor = jnp.linalg.cholesky(reduced)
    return jax.scipy.linalg.cho_solve((lower_factor, True), projected)


def shards(operator_cores, vector_cores, left_gram, bases):
    gram_now = left_gram
    results = []
    core_count = operator_cores.shape[0]
    for core_index in range(core_count):
        mixing = solve_mixing(gram_now, bases[core_index])
        next_basis = bases[core_index + 1]
        operator_core = operator_cores[core_index]
        vector_core = vector_cores[core_index]
        local_rows = vector_core.shape[0]
        vector_width = vector_core.shape[1]
        operator_width = operator_core.shape[0]
        local_modes = operator_core.shape[2]
        gathered = lax.all_gather(vector_core, "mode", axis=2, tiled=True)
        product = jnp.einsum(
            "qsj,ptij->qpist", gathered, operator_core, preferred_element_type=jnp.float32
        )
        row_major = product.reshape(
            local_rows * operator_width, local_modes, vector_width * operator_width
        )
        row_major = row_major.astype(jnp.bfloat16)
        exchanged = lax.all_to_all(row_major, "rank", split_axis=1, concat_axis=0, tiled=True)
        widened = exchanged.astype(jnp.float32)
        weighted = jnp.einsum("ad,dib->aib", gram_now, widened, precision=HIGHEST_PRECISION)
        partial_gram = jnp.einsum("aib,aic->bc", widened, weighted, precision=HIGHEST_PRECISION) / (
            MODES * RANK
        )
        mixed = jnp.einsum("sa,aib->sib", mixing, widened, precision=HIGHEST_PRECISION)
        rounded_core = jnp.einsum("sib,bt->sit", mixed, next_basis, precision=HIGHEST_PRECISION)
        results.append(rounded_core)
        gram_now = lax.psum(partial_gram, ("mode", "rank"))
    return (jnp.stack(results), gram_now)


def solution(mesh):
    placed = (P(None, None, None, "mode", None), P(None, "rank", None, "mode"), P(), P())
    return jax.shard_map(
        shards,
        mesh=mesh,
        in_specs=placed,
        out_specs=(P(None, None, ("mode", "rank"), None), P()),
        check_vma=False,
    )
```

profile of v0, /device:TPU:4, one launch (start us, length us, event | category | flops | bytes accessed | tf_op | source)
XLA Modules:
  0.0 1263.4 jit_solution(10983501923882909832)
XLA Ops:
  7.2 0.0 copy-start
  7.2 0.0 all-gather.5.cloned.1.call-start
  7.2 0.9 fusion.62
  8.1 0.7 copy.55
  8.8 0.0 all-gather.5.cloned.1.call-update
  8.8 0.0 all-gather.7.cloned.1.call-start
  8.9 0.7 copy.56
  9.5 0.0 all-gather.7.cloned.1.call-update
  9.6 0.0 copy-done
  9.6 1.1 fusion.43
  10.7 1.0 fusion.41
  11.7 0.1 copy.28
  11.8 0.1 copy.29
  11.9 5.8 cholesky.44
  17.8 0.7 compare_reduce_fusion.1
  18.5 0.6 fusion.51
  19.1 4.9 custom-call.8
  24.0 0.3 fusion.58
  24.3 0.2 convolution_bitcast_fusion.6
  24.5 138.1 %all-gather.5.cloned.1.call-done = bf16[1,8,64,2048]{2,1,0,3:T(8,128)(2,1)} async-done(((bf16[1,8,64,32]{2,1,0,3:T(8,128)(2,1)}), bf16[1,8,64,2048]{2,1,0,3:T(8,128)(2,1)}) %all-gather.5.cloned.1.call-update) | async-done | bytes 2097168 | tf_op jit(solution)/shard_map/all_gather | solution.py:36
  162.6 4.5 copy.31
  167.1 3.9 fusion.23
  171.0 1.4 copy.32
  172.4 1.8 copy.33
  174.2 4.8 all-to-all-start
  179.0 128.4 %all-gather.7.cloned.1.call-done = bf16[1,8,64,2048]{2,1,0,3:T(8,128)(2,1)} async-done(((bf16[1,8,64,32]{2,1,0,3:T(8,128)(2,1)}), bf16[1,8,64,2048]{2,1,0,3:T(8,128)(2,1)}) %all-gather.7.cloned.1.call-update) | async-done | bytes 2097168 | tf_op jit(solution)/shard_map/all_gather | solution.py:36
  307.4 4.5 copy.41
  311.8 4.9 fusion.18
  316.8 2.9 copy.42
  319.7 1.8 copy.43
  321.4 0.0 all-to-all-done
  321.4 4.8 all-to-all-start.1
  326.2 0.0 all-reduce.3.cloned.1.call-start
  326.3 0.7 convolution_bitcast_fusion
  327.0 0.0 copy-start.2
  327.0 1.5 fusion.29
  328.5 0.0 all-reduce.3.cloned.1.call-update
  328.5 0.2 all-reduce.5.cloned.1.call-start
  328.7 0.4 fusion.63
  329.1 4.3 all-to-all-done.1
  333.5 0.0 copy-done.2
  333.5 0.4 convolution_bitcast_fusion.4
  333.9 451.1 %all-reduce.3.cloned.1.call-done = f32[256,256]{1,0:T(8,128)} async-done(((f32[256,256]{1,0:T(8,128)}), f32[256,256]{1,0:T(8,128)}) %all-reduce.3.cloned.1.call-update) | async-done | bytes 262160 | tf_op jit(solution)/shard_map/psum | solution.py:53
  784.9 0.0 copy-start.1
  784.9 1.3 fusion.37
  786.2 0.2 fusion.39
  786.4 0.1 copy.38
  786.5 0.1 copy.39
  786.6 5.8 cholesky.55
  792.5 0.6 compare_reduce_fusion
  793.1 0.7 fusion.52
  793.8 4.9 custom-call.9
  798.7 0.3 fusion.34
  799.0 0.2 convolution_bitcast_fusion.5
  799.2 0.4 fusion.64
  799.6 0.0 copy-done.1
  799.6 0.6 fusion.30
  800.1 1.5 fusion.28
  801.6 0.0 all-reduce.5.cloned.1.call-update
  801.7 0.4 convolution_bitcast_fusion.3
  802.1 0.9 copy.46
  802.9 452.2 %all-reduce.5.cloned.1.call-done = f32[256,256]{1,0:T(8,128)} async-done(((f32[256,256]{1,0:T(8,128)}), f32[256,256]{1,0:T(8,128)}) %all-reduce.5.cloned.1.call-update) | async-done | bytes 262160 | tf_op jit(solution)/shard_map/psum | solution.py:53
  1255.2 1.7 copy.59
  (9 shorter events, 0.2 us)
Async XLA Ops:
  7.2 2.4 copy-start
  7.2 155.4 %all-gather.5.cloned.1.call-start = ((), (), s32[]{:S(2)}) async-start(), calls=%async_computation.4 | async-start | bytes 4259840 | tf_op jit(solution)/shard_map/all_gather | solution.py:36
  8.8 298.6 %all-gather.7.cloned.1.call-start = ((), (), s32[]{:S(2)}) async-start(), calls=%async_computation.5 | async-start | bytes 4259840 | tf_op jit(solution)/shard_map/all_gather | solution.py:36
  174.2 147.2 %all-to-all-start = ((bf16[32,32,256]{2,0,1:T(8,128)(2,1)}), bf16[32,32,256]{2,0,1:T(8,128)(2,1)S(1)}, u32[]{:S(2)}, u32[]{:S(2)}) async-start(bf16[32,32,256]{2,0,1:T(8,128)(2,1)} %copy.33), calls=%async_computation | async-start | bytes 1048576 | tf_op jit(solution)/shard_map/all_to_all | solution.py:44
  321.4 12.0 all-to-all-start.1
  326.2 458.7 %all-reduce.3.cloned.1.call-start = ((), (), s32[]{:S(2)}) async-start(), calls=%async_computation.2 | async-start | bytes 524288 | tf_op jit(solution)/shard_map/psum | solution.py:53
  327.0 6.5 copy-start.2
  328.5 926.7 %all-reduce.5.cloned.1.call-start = ((), (), s32[]{:S(2)}) async-start(), calls=%async_computation.3 | async-start | bytes 524288 | tf_op jit(solution)/shard_map/psum | solution.py:53
  784.9 14.6 %copy-start.1 = (f32[256,256]{1,0:T(8,128)S(1)}, f32[256,256]{1,0:T(8,128)}, u32[]{:S(2)}) copy-start(f32[256,256]{1,0:T(8,128)} %all-reduce.3.cloned.1.call-done) | copy-start | bytes 786436
Sparse Core Ops, SparseCore 0:
  11.5 151.0 all-gather.4
  166.1 141.1 all-gather.6
  333.1 451.7 all-reduce.2
  801.8 453.3 all-reduce.4
where the time goes:
time: 1260 us
  waiting for transfers between devices  1170 us (93%)
  other arithmetic  24.2 us (2%)
  local copies, waits for them, and re-layouts  21.9 us (2%)
  matrix products  19.1 us (2%)
  between operations  14 us (1%)
    psum x2, waiting for transfers between devices, shards(): gram_now = lax.psum(partial_gram, ('mode', 'rank'))  903 us
    all_gather x2, waiting for transfers between devices, shards(): gathered = lax.all_gather(vector_core, 'mode', axis=2, tiled=True)  267 us
  transfers between devices with their start and end apart: 6, of which 5 were waited for; matrix products, arithmetic and copies ran while one was open for 4% of the time, Pallas kernels for 0%

commit v1 on v0

--- a/solution.py
+++ b/solution.py
@@ -50,7 +50,7 @@
         mixed = jnp.einsum("sa,aib->sib", mixing, widened, precision=HIGHEST_PRECISION)
         rounded_core = jnp.einsum("sib,bt->sit", mixed, next_basis, precision=HIGHEST_PRECISION)
         results.append(rounded_core)
-        gram_now = lax.psum(partial_gram, ("mode", "rank"))
+        gram_now = lax.psum(lax.psum(partial_gram, "rank"), "mode")
     return (jnp.stack(results), gram_now)
 
 

time: 1260 us -> 1030 us (0.82)
  the two profiles are of different devices: /device:TPU:4 before, /device:TPU:2 now
where the time goes in v1:
time: 1030 us
  waiting for transfers between devices  935 us (91%)
  other arithmetic  24.1 us (2%)
  local copies, waits for them, and re-layouts  21.9 us (2%)
  matrix products  20 us (2%)
  between operations  14.3 us (1%)
    psum x4, waiting for transfers between devices, shards(): gram_now = lax.psum(lax.psum(partial_gram, 'rank'), 'mode')  662 us
    all_gather x2, waiting for transfers between devices, shards(): gathered = lax.all_gather(vector_core, 'mode', axis=2, tiled=True)  267 us
  transfers between devices with their start and end apart: 8, of which 7 were waited for; matrix products, arithmetic and copies ran while one was open for 4% of the time, Pallas kernels for 0%

profile of v1, /device:TPU:2, one launch (start us, length us, event | category | flops | bytes accessed | tf_op | source)
XLA Modules:
  0.0 1025.8 jit_solution(16663849172990208656)
XLA Ops:
  7.2 0.0 copy-start
  7.2 0.0 all-gather.5.cloned.1.call-start
  7.2 0.9 fusion.62
  8.1 0.7 copy.55
  8.8 0.0 all-gather.5.cloned.1.call-update
  8.8 0.0 all-gather.7.cloned.1.call-start
  8.9 0.7 copy.56
  9.5 0.0 all-gather.7.cloned.1.call-update
  9.6 1.1 fusion.43
  10.7 1.0 fusion.41
  11.7 0.1 copy.28
  11.8 0.1 copy.29
  11.9 5.8 cholesky.44
  17.8 0.6 compare_reduce_fusion.1
  18.5 0.6 fusion.51
  19.0 4.9 custom-call.8
  23.9 138.7 %all-gather.5.cloned.1.call-done = bf16[1,8,64,2048]{2,1,0,3:T(8,128)(2,1)} async-done(((bf16[1,8,64,32]{2,1,0,3:T(8,128)(2,1)}), bf16[1,8,64,2048]{2,1,0,3:T(8,128)(2,1)}) %all-gather.5.cloned.1.call-update) | async-done | bytes 2097168 | tf_op jit(solution)/shard_map/all_gather | solution.py:36
  162.6 4.5 copy.31
  167.1 3.9 fusion.23
  171.0 1.4 copy.32
  172.4 1.8 copy.33
  174.2 4.8 all-to-all-start
  179.0 128.4 %all-gather.7.cloned.1.call-done = bf16[1,8,64,2048]{2,1,0,3:T(8,128)(2,1)} async-done(((bf16[1,8,64,32]{2,1,0,3:T(8,128)(2,1)}), bf16[1,8,64,2048]{2,1,0,3:T(8,128)(2,1)}) %all-gather.7.cloned.1.call-update) | async-done | bytes 2097168 | tf_op jit(solution)/shard_map/all_gather | solution.py:36
  307.4 4.5 copy.41
  311.9 4.9 fusion.18
  316.8 2.9 copy.42
  319.7 1.8 copy.43
  321.4 0.0 all-to-all-done
  321.5 4.8 all-to-all-start.1
  326.3 0.7 convolution_bitcast_fusion
  327.0 0.0 copy-start.1
  327.0 1.5 fusion.29
  328.5 0.0 all-reduce.5.cloned.1.call-update
  328.5 0.0 all-reduce.7.cloned.1.call-start
  328.6 0.3 fusion.58
  328.8 0.2 convolution_bitcast_fusion.6
  329.0 6.1 all-to-all-done.1
  335.2 62.3 %all-reduce.5.cloned.1.call-done = f32[256,256]{1,0:T(8,128)} async-done(((f32[256,256]{1,0:T(8,128)}), f32[256,256]{1,0:T(8,128)}) %all-reduce.5.cloned.1.call-update) | async-done | bytes 262160 | tf_op jit(solution)/shard_map/psum | solution.py:53
  397.5 0.0 all-reduce.7.cloned.1.call-update
  397.5 0.2 all-reduce.9.cloned.1.call-start
  397.8 0.4 fusion.63
  398.2 0.4 convolution_bitcast_fusion.4
  398.5 266.7 %all-reduce.7.cloned.1.call-done = f32[256,256]{1,0:T(8,128)} async-done(((f32[256,256]{1,0:T(8,128)}), f32[256,256]{1,0:T(8,128)}) %all-reduce.7.cloned.1.call-update) | async-done | bytes 262160 | tf_op jit(solution)/shard_map/psum | solution.py:53
  665.2 1.2 fusion.37
  666.5 0.2 fusion.39
  666.7 0.1 copy.38
  666.8 0.1 copy.39
  666.9 5.8 cholesky.55
  672.7 0.6 compare_reduce_fusion
  673.4 0.7 fusion.52
  674.0 4.9 custom-call.9
  678.9 1.5 fusion.30
  680.5 1.5 fusion.28
  682.0 0.0 all-reduce.9.cloned.1.call-update
  682.0 0.0 all-reduce.11.cloned.1.call-start
  682.1 0.3 fusion.34
  682.3 0.2 convolution_bitcast_fusion.5
  682.5 67.0 %all-reduce.9.cloned.1.call-done = f32[256,256]{1,0:T(8,128)} async-done(((f32[256,256]{1,0:T(8,128)}), f32[256,256]{1,0:T(8,128)}) %all-reduce.9.cloned.1.call-update) | async-done | bytes 262160 | tf_op jit(solution)/shard_map/psum | solution.py:53
  749.5 0.0 all-reduce.11.cloned.1.call-update
  749.6 0.4 fusion.64
  749.9 0.4 convolution_bitcast_fusion.3
  750.3 0.9 copy.46
  751.2 266.0 %all-reduce.11.cloned.1.call-done = f32[256,256]{1,0:T(8,128)} async-done(((f32[256,256]{1,0:T(8,128)}), f32[256,256]{1,0:T(8,128)}) %all-reduce.11.cloned.1.call-update) | async-done | bytes 262160 | tf_op jit(solution)/shard_map/psum | solution.py:53
  1017.3 1.7 copy.61
  (12 shorter events, 0.2 us)
Async XLA Ops:
  7.2 2.4 copy-start
  7.2 155.5 %all-gather.5.cloned.1.call-start = ((), (), s32[]{:S(2)}) async-start(), calls=%async_computation.6 | async-start | bytes 4259840 | tf_op jit(solution)/shard_map/all_gather | solution.py:36
  8.8 298.6 %all-gather.7.cloned.1.call-start = ((), (), s32[]{:S(2)}) async-start(), calls=%async_computation.7 | async-start | bytes 4259840 | tf_op jit(solution)/shard_map/all_gather | solution.py:36
  174.2 147.2 %all-to-all-start = ((bf16[32,32,256]{2,0,1:T(8,128)(2,1)}), bf16[32,32,256]{2,0,1:T(8,128)(2,1)S(1)}, u32[]{:S(2)}, u32[]{:S(2)}) async-start(bf16[32,32,256]{2,0,1:T(8,128)(2,1)} %copy.33), calls=%async_computation | async-start | bytes 1048576 | tf_op jit(solution)/shard_map/all_to_all | solution.py:44
  321.5 13.7 %all-to-all-start.1 = ((bf16[32,32,256]{2,0,1:T(8,128)(2,1)}), bf16[32,32,256]{2,0,1:T(8,128)(2,1)S(1)}, u32[]{:S(2)}, u32[]{:S(2)}) async-start(bf16[32,32,256]{2,0,1:T(8,128)(2,1)} %copy.43), calls=%async_computation.1 | async-start | bytes 1048576 | tf_op jit(solution)/shard_map/all_to_all | solution.py:44
  326.3 71.3 %all-reduce.5.cloned.1.call-start = ((), (), s32[]{:S(2)}) async-start(), calls=%async_computation.2 | async-start | bytes 524288 | tf_op jit(solution)/shard_map/psum | solution.py:53
  327.0 71.1 %copy-start.1 = (f32[3,256,64]{1,2,0:T(8,128)S(1)}, f32[3,256,64]{1,2,0:T(8,128)}, u32[]{:S(2)}) copy-start(f32[3,256,64]{1,2,0:T(8,128)} %param.10) | copy-start | bytes 589828
  328.5 336.7 %all-reduce.7.cloned.1.call-start = ((), (), s32[]{:S(2)}) async-start(), calls=%async_computation.3 | async-start | bytes 524288 | tf_op jit(solution)/shard_map/psum | solution.py:53
  397.5 352.0 %all-reduce.9.cloned.1.call-start = ((), (), s32[]{:S(2)}) async-start(), calls=%async_computation.4 | async-start | bytes 524288 | tf_op jit(solution)/shard_map/psum | solution.py:53
  682.0 335.2 %all-reduce.11.cloned.1.call-start = ((), (), s32[]{:S(2)}) async-start(), calls=%async_computation.5 | async-start | bytes 524288 | tf_op jit(solution)/shard_map/psum | solution.py:53
Sparse Core Ops, SparseCore 0:
  11.5 151.0 all-gather.4
  166.2 141.1 all-gather.6
  330.0 67.4 all-reduce.4
  401.2 264.0 all-reduce.6
  682.1 67.3 all-reduce.8
  753.2 264.0 all-reduce.10

commit v2 on v0

--- a/solution.py
+++ b/solution.py
@@ -33,7 +33,9 @@
         vector_width = vector_core.shape[1]
         operator_width = operator_core.shape[0]
         local_modes = operator_core.shape[2]
-        gathered = lax.all_gather(vector_core, "mode", axis=2, tiled=True)
+        gathered = jnp.concatenate(
+            lax.all_to_all(jnp.stack([vector_core] * lax.axis_size("mode")), "mode", 0, 0), axis=2
+        )
         product = jnp.einsum(
             "qsj,ptij->qpist", gathered, operator_core, preferred_element_type=jnp.float32
         )

time: 1260 us -> 1220 us (0.968)
  waiting for transfers between devices: 1170 us -> 1070 us
  local copies, waits for them, and re-layouts: 21.9 us -> 56.4 us
  starting transfers between devices: 9.91 us -> 37.3 us
    all_gather x2 -> x0, waiting for transfers between devices: 267 us -> none  [shards(): gathered = lax.all_gather(vector_core, 'mode', axis=2, tiled=True)]
    all_to_all x0 -> x2, waiting for transfers between devices: none -> 161 us  [shards(): lax.all_to_all(jnp.stack([vector_core] * lax.axis_size('mode')), 'mode',...]
    unnamed x10 -> x16, local copies, waits for them, and re-layouts: 3.88 us -> 37.5 us
    all_to_all x0 -> x2, starting transfers between devices: none -> 27.5 us  [shards(): lax.all_to_all(jnp.stack([vector_core] * lax.axis_size('mode')), 'mode',...]
where the time goes in v2:
time: 1220 us
  waiting for transfers between devices  1070 us (88%)
  local copies, waits for them, and re-layouts  56.4 us (5%)
  starting transfers between devices  37.3 us (3%)
  other arithmetic  24.2 us (2%)
  matrix products  18 us (1%)
  between operations  14.3 us (1%)
    psum x2, waiting for transfers between devices, shards(): gram_now = lax.psum(partial_gram, ('mode', 'rank'))  902 us
    all_to_all x2, waiting for transfers between devices, shards(): lax.all_to_all(jnp.stack([vector_core] * lax.axis_size('mode')), 'mode',...  161 us
    unnamed x16, local copies, waits for them, and re-layouts  37.5 us
    all_to_all x2, starting transfers between devices, shards(): lax.all_to_all(jnp.stack([vector_core] * lax.axis_size('mode')), 'mode',...  27.5 us
  transfers between devices with their start and end apart: 6, of which 5 were waited for; matrix products, arithmetic and copies ran while one was open for 4% of the time, Pallas kernels for 0%

profile of v2, /device:TPU:4, one launch (start us, length us, event | category | flops | bytes accessed | tf_op | source)
XLA Modules:
  0.0 1217.3 jit_solution(1675432808739771378)
XLA Ops:
  7.2 0.0 copy-start
  7.2 0.9 slice_bitcast_fusion
  8.1 2.9 broadcast_bitcast_fusion
  11.1 7.9 reshape.50
  18.9 18.7 %all-to-all-start.2 = ((bf16[64,2,8192]{2,1,0:T(2,128)(2,1)}), bf16[64,2,8192]{2,1,0:T(2,128)(2,1)S(1)}, u32[]{:S(2)}, u32[]{:S(2)}) async-start(bf16[64,2,8192]{2,1,0:T(2,128)(2,1)} %reshape.50), calls=%async_computation.2 | async-start | bytes 4194304 | tf_op jit(solution)/shard_map/all_to_all | solution.py:37
  37.7 2.9 broadcast_bitcast_fusion.1
  40.6 7.9 reshape.48
  48.5 86.4 %all-to-all-done.2 = bf16[64,2,8192]{2,1,0:T(2,128)(2,1)S(1)} async-done(((bf16[64,2,8192]{2,1,0:T(2,128)(2,1)}), bf16[64,2,8192]{2,1,0:T(2,128)(2,1)S(1)}, u32[]{:S(2)}, u32[]{:S(2)}) %all-to-all-start.2) | async-done | bytes 2097184 | tf_op jit(solution)/shard_map/all_to_all | solution.py:37
  134.9 8.8 all-to-all-start
  143.8 0.2 fusion.33
  144.0 0.2 fusion.31
  144.2 0.1 copy.28
  144.3 0.1 copy.29
  144.4 5.8 cholesky.44
  150.3 0.6 compare_reduce_fusion.1
  150.9 0.7 fusion.41
  151.6 4.9 custom-call.8
  156.5 0.3 fusion.48
  156.8 0.2 convolution_bitcast_fusion.6
  157.0 4.0 reshape.51
  161.0 3.1 bitcast_bitcast_fusion
  164.1 2.8 copy.40
  166.9 74.1 %all-to-all-done = bf16[64,2,8192]{2,1,0:T(2,128)(2,1)} async-done(((bf16[64,2,8192]{2,1,0:T(2,128)(2,1)}), bf16[64,2,8192]{2,1,0:T(2,128)(2,1)}, u32[]{:S(2)}, u32[]{:S(2)}) %all-to-all-start) | async-done | bytes 2097184 | tf_op jit(solution)/shard_map/all_to_all | solution.py:37
  241.0 8.0 reshape.49
  248.9 3.1 bitcast_bitcast_fusion.1
  252.0 0.0 copy-start.3
  252.0 0.9 copy.30
  252.9 1.3 copy-done.3
  254.2 2.3 fusion.15
  256.6 1.4 copy.32
  257.9 1.8 copy.33
  259.7 4.8 all-to-all-start.1
  264.5 6.1 fusion.12
  270.6 2.9 copy.42
  273.5 1.8 copy.43
  275.3 0.0 all-to-all-done.1
  275.3 4.9 all-to-all-start.3
  280.2 0.0 all-reduce.3.cloned.1.call-start
  280.3 0.7 convolution_bitcast_fusion
  281.0 1.5 fusion.19
  282.5 0.0 all-reduce.3.cloned.1.call-update
  282.5 0.0 all-reduce.5.cloned.1.call-start
  282.5 0.4 fusion.52
  282.9 4.5 all-to-all-done.3
  287.5 0.4 convolution_bitcast_fusion.4
  287.9 450.4 %all-reduce.3.cloned.1.call-done = f32[256,256]{1,0:T(8,128)} async-done(((f32[256,256]{1,0:T(8,128)}), f32[256,256]{1,0:T(8,128)}) %all-reduce.3.cloned.1.call-update) | async-done | bytes 262160 | tf_op jit(solution)/shard_map/psum | solution.py:55
  738.2 1.2 fusion.27
  739.4 0.2 fusion.29
  739.7 0.1 copy.38
  739.7 0.1 copy.39
  739.8 5.8 cholesky.55
  745.7 0.6 compare_reduce_fusion
  746.4 0.7 fusion.42
  747.0 4.9 custom-call.9
  751.9 0.3 fusion.24
  752.2 0.2 convolution_bitcast_fusion.5
  752.4 0.4 fusion.53
  752.8 1.5 fusion.20
  754.3 1.5 fusion.18
  755.8 0.0 all-reduce.5.cloned.1.call-update
  755.9 0.4 convolution_bitcast_fusion.3
  756.3 0.9 copy.46
  757.1 451.7 %all-reduce.5.cloned.1.call-done = f32[256,256]{1,0:T(8,128)} async-done(((f32[256,256]{1,0:T(8,128)}), f32[256,256]{1,0:T(8,128)}) %all-reduce.5.cloned.1.call-update) | async-done | bytes 262160 | tf_op jit(solution)/shard_map/psum | solution.py:55
  1208.8 1.7 copy.59
  (14 shorter events, 0.2 us)
Async XLA Ops:
  7.2 136.6 %copy-start = (f32[256,256]{1,0:T(8,128)S(1)}, f32[256,256]{1,0:T(8,128)}, u32[]{:S(2)}) copy-start(f32[256,256]{1,0:T(8,128)} %param.9) | copy-start | bytes 786436
  18.9 116.0 %all-to-all-start.2 = ((bf16[64,2,8192]{2,1,0:T(2,128)(2,1)}), bf16[64,2,8192]{2,1,0:T(2,128)(2,1)S(1)}, u32[]{:S(2)}, u32[]{:S(2)}) async-start(bf16[64,2,8192]{2,1,0:T(2,128)(2,1)} %reshape.50), calls=%async_computation.2 | async-start | bytes 4194304 | tf_op jit(solution)/shard_map/all_to_all | solution.py:37
  40.6 103.1 %copy-start.1 = (f32[3,256,64]{1,2,0:T(8,128)S(1)}, f32[3,256,64]{1,2,0:T(8,128)}, u32[]{:S(2)}) copy-start(f32[3,256,64]{1,2,0:T(8,128)} %param.10) | copy-start | bytes 589828
  134.9 106.0 %all-to-all-start = ((bf16[64,2,8192]{2,1,0:T(2,128)(2,1)}), bf16[64,2,8192]{2,1,0:T(2,128)(2,1)}, u32[]{:S(2)}, u32[]{:S(2)}) async-start(bf16[64,2,8192]{2,1,0:T(2,128)(2,1)} %reshape.48), calls=%async_computation | async-start | bytes 4194304 | tf_op jit(solution)/shard_map/all_to_all | solution.py:37
  252.0 2.2 copy-start.3
  259.7 15.6 %all-to-all-start.1 = ((bf16[32,32,256]{2,0,1:T(8,128)(2,1)}), bf16[32,32,256]{2,0,1:T(8,128)(2,1)S(1)}, u32[]{:S(2)}, u32[]{:S(2)}) async-start(bf16[32,32,256]{2,0,1:T(8,128)(2,1)} %copy.33), calls=%async_computation.1 | async-start | bytes 1048576 | tf_op jit(solution)/shard_map/all_to_all | solution.py:46
  275.3 12.2 %copy-start.2 = (f32[3,256,64]{1,2,0:T(8,128)S(1)}, f32[3,256,64]{1,2,0:T(8,128)}, u32[]{:S(2)}) copy-start(f32[3,256,64]{1,2,0:T(8,128)} %param.10) | copy-start | bytes 589828
  275.3 12.1 all-to-all-start.3
  280.2 458.0 %all-reduce.3.cloned.1.call-start = ((), (), s32[]{:S(2)}) async-start(), calls=%async_computation.4 | async-start | bytes 524288 | tf_op jit(solution)/shard_map/psum | solution.py:55
  282.5 926.3 %all-reduce.5.cloned.1.call-start = ((), (), s32[]{:S(2)}) async-start(), calls=%async_computation.5 | async-start | bytes 524288 | tf_op jit(solution)/shard_map/psum | solution.py:55
Sparse Core Ops, SparseCore 0:
  287.1 451.1 all-reduce.2
  756.0 452.7 all-reduce.4
